TPU v7x, 32 devices: a whole 2x2x4 slice. The times are simulated.
32 devices in a mesh: wave: 4 (over z), tile: 8 (over y, x, core).
Axes of the slice: x: 2, y: 2, z: 4, core: 2. Of those that a mesh axis runs over, the one named last changes fastest.
Arguments:
- spectral: bfloat16 [640, 2, 64, 1281], P('wave', None, 'tile'), may hold values from -0.083496094 to 0.083496094
- legendre: bfloat16 [640, 8, 1281], P('wave'), may hold values from -0.25 to 0.25
- pair_ids: int32 [640], replicated, may hold values from 0 to 639, each once
Outputs:
- spectral_out: bfloat16 [640, 2, 64, 1281], P('wave', None, 'tile')
Inputs may be any that keep to these rules, and one draw needn't show every extreme that they name: A permutation: each pair 0 to 639 appears once; slot s of spectral, legendre and spectral_out holds wavenumbers pair_ids[s] and 1279 - pair_ids[s].
All inputs are finite; a program needn't handle non-finite values.
Results may differ from a plain program's by a relative error of at most 0.0072.
Values may be sent and summed in bfloat16 or wider, within the bound.
A program may use at most 64 MiB of HBM per device.

v0:
```python
import functools
import math
import jax
import jax.numpy as jnp
from jax import lax
from jax.sharding import PartitionSpec as P

MW = 1280
HALF_LATS = 1280
PAIRS = 640
NPTS = 5156
LANES = 128
RADIX = 32
F32 = jnp.float32
BF16 = jnp.bfloat16


def cycle_lengths(pair_number, pair_total):
    polar_cycle = pair_number * (HALF_LATS // 2) // pair_total
    cycle_index = jnp.stack([polar_cycle, HALF_LATS - 1 - polar_cycle])
    return (cycle_index, 20 + 4 * cycle_index)


def cycle_scale(cycle_index, cycle_len, lat_count):
    angles = math.pi * (cycle_index.astype(F32) + 0.5) / (2.0 * HALF_LATS)
    return 40.0 * jnp.sin(angles) / jnp.sqrt(lat_count * cycle_len.astype(F32))


def trig(wavenumbers, local_index, length):
    phase = wavenumbers[:, None] * local_index[None, :] % length[None, :]
    angles = 2.0 * math.pi * phase.astype(F32) / length[None, :].astype(F32)
    return (jnp.cos(angles), jnp.sin(angles))


def tables(local_index, length):
    outer = MW // 2 // RADIX
    a_cos, a_sin = trig(2 * RADIX * lax.iota(jnp.int32, outer), local_index, length)
    b_cos, b_sin = trig(lax.iota(jnp.int32, 2 * RADIX), local_index, length)
    pts = local_index.shape[0]
    b_cos = b_cos.reshape(RADIX, 2, pts).transpose(1, 0, 2)[:, None]
    b_sin = b_sin.reshape(RADIX, 2, pts).transpose(1, 0, 2)[:, None]
    a_cos, a_sin = (a_cos[None, :, None], a_sin[None, :, None])
    cos = (a_cos * b_cos - a_sin * b_sin).astype(BF16).reshape(2, MW // 2, pts)
    sin = (a_sin * b_cos + a_cos * b_sin).astype(BF16).reshape(2, MW // 2, pts)
    return (cos, sin)


def grid_products(grid_values):
    layer_count = grid_values.shape[0] // 4
    u, w, t, q = grid_values.astype(F32).reshape(4, layer_count, grid_values.shape[1])
    level = lax.iota(jnp.int32, layer_count)
    acc, rows = (t[layer_count - 1], [])
    rows.append(acc)
    for v in range(layer_count - 2, -1, -1):
        acc = acc + t[v]
        rows.append(acc)
    geo = jnp.stack(rows[::-1]) / math.sqrt(layer_count)
    energy = 0.5 * (u * u + w * w) + geo
    return jnp.stack([energy, u * t, w * t, u * q]).reshape(grid_values.shape).astype(BF16)


def local(spectral, legendre, pair_ids):
    slots, _, cols, row_total = spectral.shape
    lat_count = legendre.shape[1]
    tiles = lax.axis_size("tile")
    zero = jnp.zeros((), BF16)
    wave_here = lax.axis_index("wave")
    slot_ids = lax.dynamic_slice_in_dim(pair_ids, wave_here * slots, slots)
    row_index = lax.broadcasted_iota(jnp.int32, (slots, row_total), 1)
    upper = (row_index >= (MW - slot_ids)[:, None])[:, None, :]
    masked = jnp.concatenate(
        [jnp.where(upper, zero, legendre), jnp.where(upper, legendre, zero)], axis=1
    )
    spec = spectral.reshape(slots, 2 * cols, row_total)
    cycle_index, cycle_len = cycle_lengths(wave_here, lat_count // 2)
    scales = cycle_scale(cycle_index, cycle_len, lat_count)
    quarter = NPTS // 4
    step = (
        tiles * LANES // math.gcd(4, tiles) if tiles * LANES // math.gcd(4, tiles) <= 512 else 512
    )
    kpad = -(-quarter // step) * step
    k = lax.iota(jnp.int32, kpad)
    q0 = cycle_len[0] // 4
    second = k >= q0
    inside = k < quarter
    local_index = jnp.where(inside, k - jnp.where(second, q0, 0), 0)
    length = jnp.where(second, cycle_len[1], cycle_len[0])
    cos, sin = tables(local_index, length)
    half = MW // 2
    m_order = jnp.arange(MW, dtype=jnp.int32).reshape(half, 2).T
    quarter_m = half // 2
    m0, m1 = (m_order[:, :quarter_m], m_order[:, quarter_m:])
    q_of = jnp.stack([m0, MW - 1 - m1]).reshape(2, half)
    hot = (pair_ids[None, :, None] == q_of[:, None, :]).astype(BF16)
    coefficients = (
        lax.dot_general(masked, spec, (((2,), (2,)), ((0,), (0,))), preferred_element_type=F32)
        .astype(BF16)
        .reshape(slots, 2, lat_count, 2 * cols)
    )
    coefficients = coefficients.transpose(2, 1, 3, 0)
    fourier = lax.all_to_all(coefficients, "wave", split_axis=0, concat_axis=3, tiled=True)
    ordered = lax.dot_general(
        fourier, hot, (((3,), (1,)), ((1,), (0,))), preferred_element_type=F32
    )
    ordered = ordered.reshape(2, 2, 2, cols, 2, quarter_m).transpose(4, 2, 1, 3, 0, 5)
    ordered = ordered.reshape(2, 2, 2, cols, half)
    factor = jnp.where(m_order == 0, 1.0, 2.0).astype(F32)
    keep = 2 * m_order[:, None, :] < cycle_len[None, :, None]
    ordered = ordered * jnp.where(keep, factor[:, None, :], 0.0)[:, None, :, None, :]
    sign = jnp.where(m_order // 2 % 2 == 0, 1.0, -1.0).astype(F32)
    re, im = (ordered[:, 0].reshape(2, 2 * cols, half), ordered[:, 1].reshape(2, 2 * cols, half))
    even_c = jnp.concatenate([re[0], re[0] * sign[0]]).astype(BF16)
    even_s = jnp.concatenate([-im[0], -im[0] * sign[0]]).astype(BF16)
    odd_c = jnp.concatenate([re[1], im[1] * sign[1]]).astype(BF16)
    odd_s = jnp.concatenate([-im[1], re[1] * sign[1]]).astype(BF16)
    dot = functools.partial(jnp.dot, preferred_element_type=F32)
    even = (dot(even_c, cos[0]) + dot(even_s, sin[0])).reshape(2, 2, cols, kpad)
    odd = (dot(odd_c, cos[1]) + dot(odd_s, sin[1])).reshape(2, 2, cols, kpad)
    even = jnp.where(second, even[:, 1], even[:, 0])
    odd = jnp.where(second, odd[:, 1], odd[:, 0])
    grid_values = jnp.stack(
        [even[0] + odd[0], even[1] - odd[1], even[0] - odd[0], even[1] + odd[1]], axis=1
    ).astype(BF16)
    grid_values = grid_values.reshape(cols, 4 * kpad)
    grid_values = lax.all_to_all(grid_values, "tile", split_axis=1, concat_axis=0, tiled=True)
    product = grid_products(grid_values)
    product = lax.all_to_all(product, "tile", split_axis=0, concat_axis=1, tiled=True)
    x = product.astype(F32).reshape(cols, 4, kpad)
    x = jnp.where(inside, x, 0.0)
    x0, x1, x2, x3 = (x[:, 0], x[:, 1], x[:, 2], x[:, 3])

    def by_lat(a, b):
        both = jnp.stack([a, b])[:, None]
        return (
            jnp.where(second == (lax.iota(jnp.int32, 2) == 1)[None, :, None, None], both, 0.0)
            .astype(BF16)
            .reshape(4 * cols, kpad)
        )

    even_in = by_lat(x0 + x2 + (x1 + x3), x0 + x2 - (x1 + x3))
    odd_in = by_lat(x0 - x2, x1 - x3)
    nt = lambda a, b: lax.dot_general(
        a, b, (((1,), (1,)), ((), ())), preferred_element_type=F32
    ).reshape(2, 2, cols, half)
    ec, es = (nt(even_in, cos[0]), nt(even_in, sin[0]))
    oc, os_ = (nt(odd_in, cos[1]), nt(odd_in, sin[1]))
    pick = sign[0] > 0
    even_re = jnp.where(pick, ec[0], ec[1])
    even_im = -jnp.where(pick, es[0], es[1])
    odd_re = oc[0] - sign[1] * os_[1]
    odd_im = -os_[0] - sign[1] * oc[1]
    back = jnp.stack([jnp.stack([even_re, even_im]), jnp.stack([odd_re, odd_im])])
    back = back * jnp.where(keep, scales[None, :, None], 0.0)[:, None, :, None, :]
    back = back.astype(BF16).reshape(2, 2, 2, cols, 2, quarter_m).transpose(4, 2, 1, 3, 0, 5)
    back = back.reshape(2, 4 * cols, half)
    back = lax.dot_general(
        back, hot, (((2,), (2,)), ((0,), (0,))), preferred_element_type=F32
    ).astype(BF16)
    back = back.reshape(2, 2, 2 * cols, PAIRS).transpose(1, 0, 2, 3)
    returned = lax.all_to_all(back, "wave", split_axis=3, concat_axis=0, tiled=True)
    returned = returned.transpose(3, 2, 1, 0).reshape(slots, 2 * cols, 2 * lat_count)
    result = lax.dot_general(
        returned, masked, (((2,), (1,)), ((0,), (0,))), preferred_element_type=F32
    )
    return result.reshape(slots, 2, cols, row_total).astype(BF16)


def solution(mesh):
    placed = (P("wave", None, "tile", None), P("wave", None, None), P())
    return jax.shard_map(
        local, mesh=mesh, in_specs=placed, out_specs=P("wave", None, "tile", None), check_vma=False
    )
```

profile of v0, /device:TPU:0, one launch (start us, length us, event | category | flops | bytes accessed | tf_op | source)
XLA Modules:
  0.0 97.7 jit_solution(9886017591165895922)
XLA Ops:
  0.0 0.8 dynamic-slice_subtract_fusion
  1.0 5.1 %broadcast_select_fusion.1 = (bf16[160,8,1281]{2,1,0:T(8,128)(2,1)}, bf16[160,8,1281]{2,1,0:T(8,128)(2,1)}) fusion(bf16[160,8,1281]{2,1,0:T(8,128)(2,1)} %param.4, pred[160,1281]{1,0:T(8,128)(4,1)S(1)} %iota_compare_fusion), kind=kLoop, calls=%fused_computation.10 | loop fusion | flops 3279360 | bytes 10043040 | tf_op jit(solution)/shard_map/jit(_where)/select_n | solution.py:72
  6.1 8.6 %fusion.12 = bf16[160,2,8,16]{3,2,1,0:T(8,128)(2,1)S(1)} fusion(bf16[160,2,8,1281]{3,2,1,0:T(8,128)(2,1)} %param.3, bf16[160,8,1281]{2,1,0:T(8,128)(2,1)} %get-tuple-element.27, bf16[160,8,1281]{2,1,0:T(8,128)(2,1)} %get-tuple-element.26), kind=kOutput, calls=%fused_computation.19 | convolution fusion | flops 118097920 | bytes 13199360 | tf_op jit(solution)/shard_map/dot_general | solution.py:96
  14.6 1.2 %copy.44 = bf16[160,2,8,16]{0,3,1,2:T(8,128)(2,1)} copy(bf16[160,2,8,16]{3,2,1,0:T(8,128)(2,1)S(1)} %fusion.12) | data formatting | bytes 163840 | tf_op jit(solution)/shard_map/reshape | solution.py:98
  15.9 6.3 %all-to-all-start = ((bf16[8,2,16,160]{3,2,1,0:T(8,128)(2,1)}), bf16[8,2,16,160]{3,2,1,0:T(8,128)(2,1)S(1)}, u32[]{:S(2)}, u32[]{:S(2)}) async-start(bf16[8,2,16,160]{3,2,1,0:T(8,128)(2,1)} %bitcast.5), calls=%async_computation | async-start | bytes 262144 | tf_op jit(solution)/shard_map/all_to_all | solution.py:101
  25.6 1.3 %iota_compare_fusion.2 = (pred[1536]{0:T(1024)(128)(4,1)S(1)}, pred[1536]{0:T(1024)(128)(4,1)S(1)}) fusion(s32[]{:T(128)S(6)} %select_n.232, s32[]{:T(128)} %bitcast.2, s32[]{:T(128)} %bitcast.13), kind=kLoop, calls=%fused_computation.136 | loop fusion | flops 7680 | bytes 3084 | tf_op jit(solution)/shard_map/ge | solution.py:84
  26.9 1.3 %compare_select_fusion.1 = (s32[1536]{0:T(1024)S(1)}, f32[1536]{0:T(1024)S(1)}) fusion(s32[]{:T(128)} %bitcast.2, s32[]{:T(128)} %bitcast.13, s32[]{:T(128)S(6)} %select_n.232), kind=kLoop, calls=%fused_computation.123 | loop fusion | flops 7680 | bytes 12300 | tf_op jit(solution)/shard_map/jit(remainder)/jit(_where)/select_n | solution.py:30
  28.3 2.1 %fusion.39 = (f32[20,1536]{1,0:T(8,128)S(1)}, f32[20,1536]{1,0:T(8,128)S(1)}) fusion(f32[1536]{0:T(1024)S(1)} %get-tuple-element.78, pred[1536]{0:T(1024)(128)(4,1)S(1)} %get-tuple-element.80, s32[1536]{0:T(1024)S(1)} %get-tuple-element.77, s32[1536]{0:T(1024)S(1)} %subtract_select_fusion, s32[20]{0:T(128)S(1)} %iota_multiply_fusion), kind=kLoop, calls=%fused_computation.65 | loop fusion | flops 337920 | bytes 265808 | tf_op jit(solution)/shard_map/cos | solution.py:32
  30.3 5.3 %fusion.27 = (f32[2,32,1536]{2,1,0:T(8,128)S(1)}, f32[2,32,1536]{2,1,0:T(8,128)S(1)}) fusion(f32[1536]{0:T(1024)S(1)} %get-tuple-element.78, pred[1536]{0:T(1024)(128)(4,1)S(1)} %get-tuple-element.80, s32[1536]{0:T(1024)S(1)} %get-tuple-element.77, s32[1536]{0:T(1024)S(1)} %subtract_select_fusion, s32[2,32]{1,0:T(2,128)S(1)} %multiply_add_fusion.1), kind=kLoop, calls=%fused_computation.40 | loop fusion | flops 1081344 | bytes 806656 | tf_op jit(solution)/shard_map/cos | solution.py:32
  35.6 2.5 %add_convert_fusion = (bf16[2,20,32,1536]{3,2,1,0:T(8,128)(2,1)S(1)}, bf16[2,20,32,1536]{3,2,1,0:T(8,128)(2,1)S(1)}) fusion(f32[2,32,1536]{2,1,0:T(8,128)S(1)} %get-tuple-element.62, f32[20,1536]{1,0:T(8,128)S(1)} %get-tuple-element.64, f32[2,32,1536]{2,1,0:T(8,128)S(1)} %get-tuple-element.61, f32[20,1536]{1,0:T(8,128)S(1)} %get-tuple-element.63), kind=kLoop, calls=%fused_computation | loop fusion | flops 15728640 | bytes 8896512 | tf_op jit(solution)/shard_map/convert_element_type | solution.py:44
  38.1 1.5 %fusion.75 = (bf16[1,20,32,1536]{3,2,1,0:T(8,128)(2,1)}, bf16[1,20,32,1536]{3,2,1,0:T(8,128)(2,1)S(1)}) fusion(bf16[2,20,32,1536]{3,2,1,0:T(8,128)(2,1)S(1)} %get-tuple-element.28), kind=kLoop, calls=%fused_computation.178 | loop fusion | bytes 7864320 | tf_op jit(solution)/shard_map/slice | solution.py:117
  39.6 2.3 %fusion.76 = (bf16[1,20,32,1536]{3,2,1,0:T(8,128)(2,1)}, bf16[1,20,32,1536]{3,2,1,0:T(8,128)(2,1)}) fusion(bf16[2,20,32,1536]{3,2,1,0:T(8,128)(2,1)S(1)} %get-tuple-element.29), kind=kLoop, calls=%fused_computation.179 | loop fusion | bytes 7864320 | tf_op jit(solution)/shard_map/slice | solution.py:117
  42.7 0.7 fusion.4
  44.0 2.1 %fusion.43 = f32[32,1536]{1,0:T(8,128)S(1)} fusion(bf16[640,1536]{1,0:T(8,128)(2,1)} %bitcast.174, bf16[16,640]{1,0:T(8,128)(2,1)S(1)} %get-tuple-element.43, bf16[16,640]{1,0:T(8,128)(2,1)S(1)} %get-tuple-element.49), kind=kOutput, calls=%fused_computation.92 | convolution fusion | flops 62996480 | bytes 2203648 | tf_op jit(solution)/shard_map/dot_general | solution.py:117
  46.1 2.0 %fusion.50 = f32[32,1536]{1,0:T(8,128)S(1)} fusion(bf16[640,1536]{1,0:T(8,128)(2,1)} %bitcast.170, bf16[16,640]{1,0:T(8,128)(2,1)S(1)} %get-tuple-element.47, bf16[16,640]{1,0:T(8,128)(2,1)S(1)} %get-tuple-element.50), kind=kOutput, calls=%fused_computation.99 | convolution fusion | flops 62996480 | bytes 2203648 | tf_op jit(solution)/shard_map/dot_general | solution.py:118
  49.8 3.7 %all-to-all-start.1 = ((bf16[8,8,768]{2,0,1:T(8,128)(2,1)}), bf16[8,8,768]{2,0,1:T(8,128)(2,1)S(1)}, u32[]{:S(2)}, u32[]{:S(2)}) async-start(bf16[8,8,768]{2,0,1:T(8,128)(2,1)} %bitcast.31), calls=%async_computation.1 | async-start | bytes 196608 | tf_op jit(solution)/shard_map/all_to_all | solution.py:125
  53.6 5.1 %all-to-all-done.1 = bf16[8,8,768]{2,0,1:T(8,128)(2,1)S(1)} async-done(((bf16[8,8,768]{2,0,1:T(8,128)(2,1)}), bf16[8,8,768]{2,0,1:T(8,128)(2,1)S(1)}, u32[]{:S(2)}, u32[]{:S(2)}) %all-to-all-start.1) | async-done | bytes 98336 | tf_op jit(solution)/shard_map/all_to_all | solution.py:125
  59.6 3.4 %all-to-all-start.2 = ((bf16[8,8,768]{2,1,0:T(8,128)(2,1)}), bf16[8,8,768]{2,1,0:T(8,128)(2,1)S(1)}, u32[]{:S(2)}, u32[]{:S(2)}) async-start(bf16[8,8,768]{2,1,0:T(8,128)(2,1)} %bitcast.40), calls=%async_computation.2 | async-start | bytes 196608 | tf_op jit(solution)/shard_map/all_to_all | solution.py:127
  62.9 5.1 %all-to-all-done.2 = bf16[8,8,768]{2,1,0:T(8,128)(2,1)S(1)} async-done(((bf16[8,8,768]{2,1,0:T(8,128)(2,1)}), bf16[8,8,768]{2,1,0:T(8,128)(2,1)S(1)}, u32[]{:S(2)}, u32[]{:S(2)}) %all-to-all-start.2) | async-done | bytes 98336 | tf_op jit(solution)/shard_map/all_to_all | solution.py:127
  68.2 2.3 %fusion.84 = f32[32,640]{1,0:T(8,128)S(1)} fusion(bf16[32,1536]{1,0:T(8,128)(2,1)S(1)} %bitcast.179, bf16[640,1536]{1,0:T(8,128)(2,1)} %bitcast.172), kind=kOutput, calls=%fused_computation.188 | convolution fusion | flops 62914560 | bytes 2146304 | tf_op jit(solution)/shard_map/dot_general | solution.py:142
  74.7 0.9 copy.54
  76.7 10.7 %all_to_all.56 = bf16[4,2,5120]{2,1,0:T(2,128)(2,1)S(1)} all-to-all(bf16[4,2,5120]{2,1,0:T(2,128)(2,1)S(1)} %reshape.950), channel_id=1, replica_groups=mesh['wave'=4,'tile'=8] {'wave'}, dimensions={0} | all-to-all | bytes 163840 | tf_op jit(solution)/shard_map/all_to_all | solution.py:160
  87.8 0.9 copy.60
  89.4 8.3 %convert_bitcast_fusion = bf16[160,2,8,1281]{3,2,1,0:T(8,128)(2,1)} fusion(bf16[160,16,16]{2,1,0:T(8,128)(2,1)S(1)} %copy.58, bf16[160,8,1281]{2,1,0:T(8,128)(2,1)} %get-tuple-element.27, bf16[160,8,1281]{2,1,0:T(8,128)(2,1)} %get-tuple-element.26), kind=kOutput, calls=%fused_computation.5 | convolution fusion | flops 121336320 | bytes 13199360 | tf_op jit(solution)/shard_map/dot_general | solution.py:162
  (89 shorter events, 11.4 us)
Async XLA Ops:
  15.9 26.6 %all-to-all-start = ((bf16[8,2,16,160]{3,2,1,0:T(8,128)(2,1)}), bf16[8,2,16,160]{3,2,1,0:T(8,128)(2,1)S(1)}, u32[]{:S(2)}, u32[]{:S(2)}) async-start(bf16[8,2,16,160]{3,2,1,0:T(8,128)(2,1)} %bitcast.5), calls=%async_computation | async-start | bytes 262144 | tf_op jit(solution)/shard_map/all_to_all | solution.py:101
  39.6 3.0 %copy-start.3 = (s32[640]{0:T(1024)S(1)}, s32[640]{0:T(1024)}, u32[]{:S(2)}) copy-start(s32[640]{0:T(1024)} %param.5) | copy-start | bytes 7684
  43.9 4.2 %copy-start.1 = (bf16[1,20,32,1536]{3,2,1,0:T(8,128)(2,1)S(1)}, bf16[1,20,32,1536]{3,2,1,0:T(8,128)(2,1)}, u32[]{:S(2)}) copy-start(bf16[1,20,32,1536]{3,2,1,0:T(8,128)(2,1)} %get-tuple-element.22) | copy-start | bytes 5898244
  49.8 8.9 %all-to-all-start.1 = ((bf16[8,8,768]{2,0,1:T(8,128)(2,1)}), bf16[8,8,768]{2,0,1:T(8,128)(2,1)S(1)}, u32[]{:S(2)}, u32[]{:S(2)}) async-start(bf16[8,8,768]{2,0,1:T(8,128)(2,1)} %bitcast.31), calls=%async_computation.1 | async-start | bytes 196608 | tf_op jit(solution)/shard_map/all_to_all | solution.py:125
  59.6 8.5 %all-to-all-start.2 = ((bf16[8,8,768]{2,1,0:T(8,128)(2,1)}), bf16[8,8,768]{2,1,0:T(8,128)(2,1)S(1)}, u32[]{:S(2)}, u32[]{:S(2)}) async-start(bf16[8,8,768]{2,1,0:T(8,128)(2,1)} %bitcast.40), calls=%async_computation.2 | async-start | bytes 196608 | tf_op jit(solution)/shard_map/all_to_all | solution.py:127
  68.0 2.5 %copy-start.2 = (bf16[1,20,32,1536]{3,2,1,0:T(8,128)(2,1)S(1)}, bf16[1,20,32,1536]{3,2,1,0:T(8,128)(2,1)}, u32[]{:S(2)}) copy-start(bf16[1,20,32,1536]{3,2,1,0:T(8,128)(2,1)} %get-tuple-element.24) | copy-start | bytes 5898244
  68.1 3.8 %copy-start = (bf16[1,20,32,1536]{3,2,1,0:T(8,128)(2,1)S(1)}, bf16[1,20,32,1536]{3,2,1,0:T(8,128)(2,1)}, u32[]{:S(2)}) copy-start(bf16[1,20,32,1536]{3,2,1,0:T(8,128)(2,1)} %get-tuple-element.25) | copy-start | bytes 5898244
where the time goes:
time: 98.3 us; the launch traced here: 97.7 us
  matrix products  27.7 us (28%)
  other arithmetic  20.9 us (21%)
  starting transfers between devices  13.4 us (14%)
  local copies, waits for them, and re-layouts  11.9 us (12%)
  blocking collectives  10.7 us (11%)
  waiting for transfers between devices  10.2 us (10%)
  between operations  3 us (3%)
    all_to_all x1, blocking collectives, local(): lax.all_to_all(back, 'wave', split_axis=3, concat_axis=0, tiled=True)  10.7 us
    dot_general x1, matrix products, local(): lax.dot_general(masked, spec, (((2,), (2,)), ((0,), (0,))), preferred_ele...  8.57 us
    dot_general x1, matrix products, local(): lax.dot_general(returned, masked, (((2,), (1,)), ((0,), (0,))), preferred...  8.31 us
    cos x2, other arithmetic, trig(): return (jnp.cos(angles), jnp.sin(angles))  7.33 us
    all_to_all x1, starting transfers between devices, local(): lax.all_to_all(coefficients, 'wave', split_axis=0, concat_axis=3, tiled=T...  6.35 us
    all_to_all x1, waiting for transfers between devices, local(): lax.all_to_all(product, 'tile', split_axis=0, concat_axis=1, tiled=True)  5.11 us
    select_n x1, other arithmetic, local(): jnp.where(upper, zero, legendre)  5.11 us
    all_to_all x1, waiting for transfers between devices, local(): lax.all_to_all(grid_values, 'tile', split_axis=1, concat_axis=0, tiled=True)  5.08 us
  transfers between devices with their start and end apart: 3, of which 2 were waited for; matrix products, arithmetic and copies ran while one was open for 18% of the time, Pallas kernels for 0%

commit v1 on v0

--- a/solution.py
+++ b/solution.py
@@ -13,6 +13,17 @@
 RADIX = 32
 F32 = jnp.float32
 BF16 = jnp.bfloat16
+
+
+def cut_along(x, dim, length):
+    before, after = (x.shape[:dim], x.shape[dim + 1 :])
+    return jnp.moveaxis(x.reshape(*before, length, -1, *after), dim, 0)
+
+
+def joined_along(blocks, dim):
+    blocks = jnp.moveaxis(blocks, 0, dim)
+    shape = blocks.shape
+    return blocks.reshape(*shape[:dim], shape[dim] * shape[dim + 1], *shape[dim + 2 :])
 
 
 def cycle_lengths(pair_number, pair_total):
@@ -157,7 +168,14 @@
         back, hot, (((2,), (2,)), ((0,), (0,))), preferred_element_type=F32
     ).astype(BF16)
     back = back.reshape(2, 2, 2 * cols, PAIRS).transpose(1, 0, 2, 3)
-    returned = lax.all_to_all(back, "wave", split_axis=3, concat_axis=0, tiled=True)
+    size, index = (lax.axis_size("wave"), lax.axis_index("wave"))
+    parts = cut_along(back, 3, size)
+    finished = [parts[index]]
+    for step_2 in range(1, size):
+        sent = parts[(index + step_2) % size]
+        finished.append(lax.ppermute(sent, "wave", [(i, (i + step_2) % size) for i in range(size)]))
+    parts = jnp.stack(finished)[(index - jnp.arange(size)) % size]
+    returned = joined_along(parts, 0)
     returned = returned.transpose(3, 2, 1, 0).reshape(slots, 2 * cols, 2 * lat_count)
     result = lax.dot_general(
         returned, masked, (((2,), (1,)), ((0,), (0,))), preferred_element_type=F32

time: 98.3 us -> 94.4 us (0.960)
  blocking collectives: 10.7 us -> 0 us
  starting transfers between devices: 13.4 us -> 19.3 us
  waiting for transfers between devices: 10.2 us -> 12.7 us
  local copies, waits for them, and re-layouts: 11.9 us -> 9.55 us
    all_to_all x1 -> x0, blocking collectives: 10.7 us -> none  [local(): lax.all_to_all(back, 'wave', split_axis=3, concat_axis=0, tiled=True)]
    ppermute x0 -> x3, starting transfers between devices: none -> 5.91 us  [local(): lax.ppermute(sent, 'wave', [(i, (i + step_2) % size) for i in range(size)])]
    ppermute x0 -> x3, waiting for transfers between devices: none -> 2.42 us  [local(): lax.ppermute(sent, 'wave', [(i, (i + step_2) % size) for i in range(size)])]
    unnamed x12 -> x13, local copies, waits for them, and re-layouts: 1.62 us -> 0.05 us
  transfers between devices with their start and end apart: 3 -> 6, of which waited for: 2 -> 4; matrix products, arithmetic and copies ran while one was open for 18% -> 19% of each run, Pallas kernels for 0% -> 0%
where the time goes in v1:
time: 94.4 us; the launch traced here: 93.9 us
  matrix products  27.7 us (29%)
  other arithmetic  21.3 us (23%)
  starting transfers between devices  19.3 us (20%)
  waiting for transfers between devices  12.7 us (13%)
  local copies, waits for them, and re-layouts  9.55 us (10%)
  between operations  3.35 us (4%)
    dot_general x1, matrix products, local(): lax.dot_general(masked, spec, (((2,), (2,)), ((0,), (0,))), preferred_ele...  8.57 us
    dot_general x1, matrix products, local(): lax.dot_general(returned, masked, (((2,), (1,)), ((0,), (0,))), preferred...  8.31 us
    cos x2, other arithmetic, trig(): return (jnp.cos(angles), jnp.sin(angles))  7.33 us
    all_to_all x1, starting transfers between devices, local(): lax.all_to_all(coefficients, 'wave', split_axis=0, concat_axis=3, tiled=T...  6.35 us
    ppermute x3, starting transfers between devices, local(): lax.ppermute(sent, 'wave', [(i, (i + step_2) % size) for i in range(size)])  5.91 us
    all_to_all x1, waiting for transfers between devices, local(): lax.all_to_all(grid_values, 'tile', split_axis=1, concat_axis=0, tiled=True)  5.19 us
    select_n x1, other arithmetic, local(): jnp.where(upper, zero, legendre)  5.11 us
    all_to_all x1, waiting for transfers between devices, local(): lax.all_to_all(product, 'tile', split_axis=0, concat_axis=1, tiled=True)  5.11 us
  transfers between devices with their start and end apart: 6, of which 4 were waited for; matrix products, arithmetic and copies ran while one was open for 19% of the time, Pallas kernels for 0%

profile of v1, /device:TPU:0, one launch (start us, length us, event | category | flops | bytes accessed | tf_op | source)
XLA Modules:
  0.0 93.9 jit_solution(15574525387759677815)
XLA Ops:
  1.0 5.1 %broadcast_select_fusion.1 = (bf16[160,8,1281]{2,1,0:T(8,128)(2,1)}, bf16[160,8,1281]{2,1,0:T(8,128)(2,1)}) fusion(bf16[160,8,1281]{2,1,0:T(8,128)(2,1)} %param.4, pred[160,1281]{1,0:T(8,128)(4,1)S(1)} %iota_compare_fusion), kind=kLoop, calls=%fused_computation.11 | loop fusion | flops 3279360 | bytes 10043040 | tf_op jit(solution)/shard_map/jit(_where)/select_n | solution.py:83
  6.1 8.6 %fusion.12 = bf16[160,2,8,16]{3,2,1,0:T(8,128)(2,1)S(1)} fusion(bf16[160,2,8,1281]{3,2,1,0:T(8,128)(2,1)} %param.3, bf16[160,8,1281]{2,1,0:T(8,128)(2,1)} %get-tuple-element.27, bf16[160,8,1281]{2,1,0:T(8,128)(2,1)} %get-tuple-element.26), kind=kOutput, calls=%fused_computation.20 | convolution fusion | flops 118097920 | bytes 13199360 | tf_op jit(solution)/shard_map/dot_general | solution.py:107
  14.6 1.2 %copy.42 = bf16[160,2,8,16]{0,3,1,2:T(8,128)(2,1)} copy(bf16[160,2,8,16]{3,2,1,0:T(8,128)(2,1)S(1)} %fusion.12) | data formatting | bytes 163840 | tf_op jit(solution)/shard_map/reshape | solution.py:109
  15.9 6.3 %all-to-all-start = ((bf16[8,2,16,160]{3,2,1,0:T(8,128)(2,1)}), bf16[8,2,16,160]{3,2,1,0:T(8,128)(2,1)S(1)}, u32[]{:S(2)}, u32[]{:S(2)}) async-start(bf16[8,2,16,160]{3,2,1,0:T(8,128)(2,1)} %bitcast.5), calls=%async_computation | async-start | bytes 262144 | tf_op jit(solution)/shard_map/all_to_all | solution.py:112
  25.9 1.3 %iota_compare_fusion.2 = (pred[1536]{0:T(1024)(128)(4,1)S(1)}, pred[1536]{0:T(1024)(128)(4,1)S(1)}) fusion(s32[]{:T(128)S(6)} %select_n.281, s32[]{:T(128)} %bitcast.2, s32[]{:T(128)} %bitcast.13), kind=kLoop, calls=%fused_computation.143 | loop fusion | flops 7680 | bytes 3084 | tf_op jit(solution)/shard_map/ge | solution.py:95
  27.3 1.3 %compare_select_fusion.1 = (s32[1536]{0:T(1024)S(1)}, f32[1536]{0:T(1024)S(1)}) fusion(s32[]{:T(128)} %bitcast.2, s32[]{:T(128)} %bitcast.13, s32[]{:T(128)S(6)} %select_n.281), kind=kLoop, calls=%fused_computation.130 | loop fusion | flops 7680 | bytes 12300 | tf_op jit(solution)/shard_map/jit(remainder)/jit(_where)/select_n | solution.py:41
  28.7 2.1 %fusion.39 = (f32[20,1536]{1,0:T(8,128)S(1)}, f32[20,1536]{1,0:T(8,128)S(1)}) fusion(f32[1536]{0:T(1024)S(1)} %get-tuple-element.82, pred[1536]{0:T(1024)(128)(4,1)S(1)} %get-tuple-element.84, s32[1536]{0:T(1024)S(1)} %get-tuple-element.81, s32[1536]{0:T(1024)S(1)} %subtract_select_fusion, s32[20]{0:T(128)S(1)} %iota_multiply_fusion), kind=kLoop, calls=%fused_computation.68 | loop fusion | flops 337920 | bytes 265808 | tf_op jit(solution)/shard_map/cos | solution.py:43
  30.8 5.3 %fusion.27 = (f32[2,32,1536]{2,1,0:T(8,128)S(1)}, f32[2,32,1536]{2,1,0:T(8,128)S(1)}) fusion(f32[1536]{0:T(1024)S(1)} %get-tuple-element.82, pred[1536]{0:T(1024)(128)(4,1)S(1)} %get-tuple-element.84, s32[1536]{0:T(1024)S(1)} %get-tuple-element.81, s32[1536]{0:T(1024)S(1)} %subtract_select_fusion, s32[2,32]{1,0:T(2,128)S(1)} %multiply_add_fusion.1), kind=kLoop, calls=%fused_computation.41 | loop fusion | flops 1081344 | bytes 806656 | tf_op jit(solution)/shard_map/cos | solution.py:43
  36.1 2.7 %add_convert_fusion = (bf16[2,20,32,1536]{3,2,1,0:T(8,128)(2,1)S(1)}, bf16[2,20,32,1536]{3,2,1,0:T(8,128)(2,1)S(1)}) fusion(f32[2,32,1536]{2,1,0:T(8,128)S(1)} %get-tuple-element.66, f32[20,1536]{1,0:T(8,128)S(1)} %get-tuple-element.68, f32[2,32,1536]{2,1,0:T(8,128)S(1)} %get-tuple-element.65, f32[20,1536]{1,0:T(8,128)S(1)} %get-tuple-element.67), kind=kLoop, calls=%fused_computation.1 | loop fusion | flops 15728640 | bytes 8896512 | tf_op jit(solution)/shard_map/convert_element_type | solution.py:55
  38.8 1.5 %fusion.77 = (bf16[1,20,32,1536]{3,2,1,0:T(8,128)(2,1)}, bf16[1,20,32,1536]{3,2,1,0:T(8,128)(2,1)S(1)}) fusion(bf16[2,20,32,1536]{3,2,1,0:T(8,128)(2,1)S(1)} %get-tuple-element.28), kind=kLoop, calls=%fused_computation.196 | loop fusion | bytes 7864320 | tf_op jit(solution)/shard_map/slice | solution.py:128
  40.3 2.3 %fusion.78 = (bf16[1,20,32,1536]{3,2,1,0:T(8,128)(2,1)}, bf16[1,20,32,1536]{3,2,1,0:T(8,128)(2,1)}) fusion(bf16[2,20,32,1536]{3,2,1,0:T(8,128)(2,1)S(1)} %get-tuple-element.29), kind=kLoop, calls=%fused_computation.197 | loop fusion | bytes 7864320 | tf_op jit(solution)/shard_map/slice | solution.py:128
  44.8 2.1 %fusion.43 = f32[32,1536]{1,0:T(8,128)S(1)} fusion(bf16[640,1536]{1,0:T(8,128)(2,1)} %bitcast.189, bf16[16,640]{1,0:T(8,128)(2,1)S(1)} %get-tuple-element.43, bf16[16,640]{1,0:T(8,128)(2,1)S(1)} %get-tuple-element.49), kind=kOutput, calls=%fused_computation.95 | convolution fusion | flops 62996480 | bytes 2203648 | tf_op jit(solution)/shard_map/dot_general | solution.py:128
  46.9 2.0 %fusion.50 = f32[32,1536]{1,0:T(8,128)S(1)} fusion(bf16[640,1536]{1,0:T(8,128)(2,1)} %bitcast.185, bf16[16,640]{1,0:T(8,128)(2,1)S(1)} %get-tuple-element.47, bf16[16,640]{1,0:T(8,128)(2,1)S(1)} %get-tuple-element.50), kind=kOutput, calls=%fused_computation.102 | convolution fusion | flops 62996480 | bytes 2203648 | tf_op jit(solution)/shard_map/dot_general | solution.py:129
  50.6 3.7 %all-to-all-start.1 = ((bf16[8,8,768]{2,0,1:T(8,128)(2,1)}), bf16[8,8,768]{2,0,1:T(8,128)(2,1)S(1)}, u32[]{:S(2)}, u32[]{:S(2)}) async-start(bf16[8,8,768]{2,0,1:T(8,128)(2,1)} %bitcast.31), calls=%async_computation.1 | async-start | bytes 196608 | tf_op jit(solution)/shard_map/all_to_all | solution.py:136
  54.3 5.2 %all-to-all-done.1 = bf16[8,8,768]{2,0,1:T(8,128)(2,1)S(1)} async-done(((bf16[8,8,768]{2,0,1:T(8,128)(2,1)}), bf16[8,8,768]{2,0,1:T(8,128)(2,1)S(1)}, u32[]{:S(2)}, u32[]{:S(2)}) %all-to-all-start.1) | async-done | bytes 98336 | tf_op jit(solution)/shard_map/all_to_all | solution.py:136
  60.4 3.4 %all-to-all-start.2 = ((bf16[8,8,768]{2,1,0:T(8,128)(2,1)}), bf16[8,8,768]{2,1,0:T(8,128)(2,1)S(1)}, u32[]{:S(2)}, u32[]{:S(2)}) async-start(bf16[8,8,768]{2,1,0:T(8,128)(2,1)} %bitcast.40), calls=%async_computation.2 | async-start | bytes 196608 | tf_op jit(solution)/shard_map/all_to_all | solution.py:138
  63.7 5.1 %all-to-all-done.2 = bf16[8,8,768]{2,1,0:T(8,128)(2,1)S(1)} async-done(((bf16[8,8,768]{2,1,0:T(8,128)(2,1)}), bf16[8,8,768]{2,1,0:T(8,128)(2,1)S(1)}, u32[]{:S(2)}, u32[]{:S(2)}) %all-to-all-start.2) | async-done | bytes 98336 | tf_op jit(solution)/shard_map/all_to_all | solution.py:138
  69.0 2.3 %fusion.86 = f32[32,640]{1,0:T(8,128)S(1)} fusion(bf16[32,1536]{1,0:T(8,128)(2,1)S(1)} %bitcast.193, bf16[640,1536]{1,0:T(8,128)(2,1)} %bitcast.187), kind=kOutput, calls=%fused_computation.205 | convolution fusion | flops 62914560 | bytes 2146304 | tf_op jit(solution)/shard_map/dot_general | solution.py:153
  76.0 2.1 %collective-permute-start = (bf16[2,2,16,160]{3,2,1,0:T(8,128)(2,1)S(1)}, bf16[2,2,16,160]{3,2,1,0:T(8,128)(2,1)S(1)}, u32[]{:S(2)}, u32[]{:S(2)}) collective-permute-start(bf16[2,2,16,160]{3,2,1,0:T(8,128)(2,1)S(1)} %bitcast.215), channel_id=1, source_target_pairs={{0,8},{8,16},{16,24},{24,0},{1,9},{9,17},{17,25},{25,1},{2,10},{10... | collective-permute-start | bytes 61448 | tf_op jit(solution)/shard_map/ppermute | solution.py:176
  78.1 2.4 %collective-permute-start.1 = (bf16[2,2,16,160]{3,2,1,0:T(8,128)(2,1)S(1)}, bf16[2,2,16,160]{3,2,1,0:T(8,128)(2,1)S(1)}, u32[]{:S(2)}, u32[]{:S(2)}) collective-permute-start(bf16[2,2,16,160]{3,2,1,0:T(8,128)(2,1)S(1)} %bitcast.214), channel_id=1, source_target_pairs={{0,16},{8,24},{16,0},{24,8},{1,17},{9,25},{17,1},{25,9},{2,18},{10... | collective-permute-start | bytes 61448 | tf_op jit(solution)/shard_map/ppermute | solution.py:176
  80.4 1.5 %collective-permute-start.2 = (bf16[2,2,16,160]{3,2,1,0:T(8,128)(2,1)S(1)}, bf16[2,2,16,160]{3,2,1,0:T(8,128)(2,1)S(1)}, u32[]{:S(2)}, u32[]{:S(2)}) collective-permute-start(bf16[2,2,16,160]{3,2,1,0:T(8,128)(2,1)S(1)} %bitcast.213), channel_id=1, source_target_pairs={{0,24},{8,0},{16,8},{24,16},{1,25},{9,1},{17,9},{25,17},{2,26},{10... | collective-permute-start | bytes 61448 | tf_op jit(solution)/shard_map/ppermute | solution.py:176
  81.9 1.0 %collective-permute-done.1 = bf16[2,2,16,160]{3,2,1,0:T(8,128)(2,1)S(1)} collective-permute-done((bf16[2,2,16,160]{3,2,1,0:T(8,128)(2,1)S(1)}, bf16[2,2,16,160]{3,2,1,0:T(8,128)(2,1)S(1)}, u32[]{:S(2)}, u32[]{:S(2)}) %collective-permute-start.1) | collective-permute-done | bytes 20512 | tf_op jit(solution)/shard_map/ppermute | solution.py:176
  82.9 1.5 %collective-permute-done.2 = bf16[2,2,16,160]{3,2,1,0:T(8,128)(2,1)S(1)} collective-permute-done((bf16[2,2,16,160]{3,2,1,0:T(8,128)(2,1)S(1)}, bf16[2,2,16,160]{3,2,1,0:T(8,128)(2,1)S(1)}, u32[]{:S(2)}, u32[]{:S(2)}) %collective-permute-start.2) | collective-permute-done | bytes 20512 | tf_op jit(solution)/shard_map/ppermute | solution.py:176
  85.6 8.3 %convert_bitcast_fusion = bf16[160,2,8,1281]{3,2,1,0:T(8,128)(2,1)} fusion(bf16[160,16,16]{2,1,0:T(8,128)(2,1)S(1)} %copy.54, bf16[160,8,1281]{2,1,0:T(8,128)(2,1)} %get-tuple-element.27, bf16[160,8,1281]{2,1,0:T(8,128)(2,1)} %get-tuple-element.26), kind=kOutput, calls=%fused_computation.6 | convolution fusion | flops 121336320 | bytes 13199360 | tf_op jit(solution)/shard_map/dot_general | solution.py:180
  (99 shorter events, 12.3 us)
Async XLA Ops:
  15.9 27.4 %all-to-all-start = ((bf16[8,2,16,160]{3,2,1,0:T(8,128)(2,1)}), bf16[8,2,16,160]{3,2,1,0:T(8,128)(2,1)S(1)}, u32[]{:S(2)}, u32[]{:S(2)}) async-start(bf16[8,2,16,160]{3,2,1,0:T(8,128)(2,1)} %bitcast.5), calls=%async_computation | async-start | bytes 262144 | tf_op jit(solution)/shard_map/all_to_all | solution.py:112
  40.3 3.2 %copy-start.3 = (s32[640]{0:T(1024)S(1)}, s32[640]{0:T(1024)}, u32[]{:S(2)}) copy-start(s32[640]{0:T(1024)} %param.5) | copy-start | bytes 7684
  44.7 4.2 %copy-start.1 = (bf16[1,20,32,1536]{3,2,1,0:T(8,128)(2,1)S(1)}, bf16[1,20,32,1536]{3,2,1,0:T(8,128)(2,1)}, u32[]{:S(2)}) copy-start(bf16[1,20,32,1536]{3,2,1,0:T(8,128)(2,1)} %get-tuple-element.22) | copy-start | bytes 5898244
  50.6 8.9 %all-to-all-start.1 = ((bf16[8,8,768]{2,0,1:T(8,128)(2,1)}), bf16[8,8,768]{2,0,1:T(8,128)(2,1)S(1)}, u32[]{:S(2)}, u32[]{:S(2)}) async-start(bf16[8,8,768]{2,0,1:T(8,128)(2,1)} %bitcast.31), calls=%async_computation.1 | async-start | bytes 196608 | tf_op jit(solution)/shard_map/all_to_all | solution.py:136
  60.4 8.5 %all-to-all-start.2 = ((bf16[8,8,768]{2,1,0:T(8,128)(2,1)}), bf16[8,8,768]{2,1,0:T(8,128)(2,1)S(1)}, u32[]{:S(2)}, u32[]{:S(2)}) async-start(bf16[8,8,768]{2,1,0:T(8,128)(2,1)} %bitcast.40), calls=%async_computation.2 | async-start | bytes 196608 | tf_op jit(solution)/shard_map/all_to_all | solution.py:138
  68.9 2.5 %copy-start.2 = (bf16[1,20,32,1536]{3,2,1,0:T(8,128)(2,1)S(1)}, bf16[1,20,32,1536]{3,2,1,0:T(8,128)(2,1)}, u32[]{:S(2)}) copy-start(bf16[1,20,32,1536]{3,2,1,0:T(8,128)(2,1)} %get-tuple-element.24) | copy-start | bytes 5898244
  68.9 3.8 %copy-start = (bf16[1,20,32,1536]{3,2,1,0:T(8,128)(2,1)S(1)}, bf16[1,20,32,1536]{3,2,1,0:T(8,128)(2,1)}, u32[]{:S(2)}) copy-start(bf16[1,20,32,1536]{3,2,1,0:T(8,128)(2,1)} %get-tuple-element.25) | copy-start | bytes 5898244
  76.0 5.9 %collective-permute-start = (bf16[2,2,16,160]{3,2,1,0:T(8,128)(2,1)S(1)}, bf16[2,2,16,160]{3,2,1,0:T(8,128)(2,1)S(1)}, u32[]{:S(2)}, u32[]{:S(2)}) collective-permute-start(bf16[2,2,16,160]{3,2,1,0:T(8,128)(2,1)S(1)} %bitcast.215), channel_id=1, source_target_pairs={{0,8},{8,16},{16,24},{24,0},{1,9},{9,17},{17,25},{25,1},{2,10},{10... | collective-permute-start | bytes 61448 | tf_op jit(solution)/shard_map/ppermute | solution.py:176
  78.1 4.8 %collective-permute-start.1 = (bf16[2,2,16,160]{3,2,1,0:T(8,128)(2,1)S(1)}, bf16[2,2,16,160]{3,2,1,0:T(8,128)(2,1)S(1)}, u32[]{:S(2)}, u32[]{:S(2)}) collective-permute-start(bf16[2,2,16,160]{3,2,1,0:T(8,128)(2,1)S(1)} %bitcast.214), channel_id=1, source_target_pairs={{0,16},{8,24},{16,0},{24,8},{1,17},{9,25},{17,1},{25,9},{2,18},{10... | collective-permute-start | bytes 61448 | tf_op jit(solution)/shard_map/ppermute | solution.py:176
  80.4 3.9 %collective-permute-start.2 = (bf16[2,2,16,160]{3,2,1,0:T(8,128)(2,1)S(1)}, bf16[2,2,16,160]{3,2,1,0:T(8,128)(2,1)S(1)}, u32[]{:S(2)}, u32[]{:S(2)}) collective-permute-start(bf16[2,2,16,160]{3,2,1,0:T(8,128)(2,1)S(1)} %bitcast.213), channel_id=1, source_target_pairs={{0,24},{8,0},{16,8},{24,16},{1,25},{9,1},{17,9},{25,17},{2,26},{10... | collective-permute-start | bytes 61448 | tf_op jit(solution)/shard_map/ppermute | solution.py:176
